TPU v7x, 32 devices: a whole 2x2x4 slice. The times are simulated.
32 devices in a mesh: cp: 4 (over y, x), grp: 8 (over z, core).
Axes of the slice: x: 2, y: 2, z: 4, core: 2. Of those that a mesh axis runs over, the one named last changes fastest.
Arguments:
- queries: bfloat16 [16, 512, 2048], P('grp', 'cp'), may hold values from -108 to 108
- keys: bfloat16 [16, 512, 2048], P('grp', 'cp'), may hold values from -4 to 4
- values: bfloat16 [16, 512, 2048], P('grp', 'cp'), may hold values from -6 to 6
- lengths: int32 [16], P('grp'), may hold values from 128 to 512
- frame_map: bfloat16 [2048, 2176], replicated, may hold values from -0.125 to 0.125
- proj_weight: bfloat16 [2176, 4096], P('grp', 'cp'), may hold values from -0.125 to 0.125
- head_weight: bfloat16 [4096, 256], P('cp'), may hold values from -0.375 to 0.375
- act_embed: float32 [7, 4096], P(None, 'cp'), may hold values from -0.5 to 0.5
- actions: int32 [16, 7], P('grp'), may hold values from 0 to 255
- action_mask: int32 [16, 7], P('grp'), may hold values 0 or 1
- group_ids: int32 [16], P('grp'), may hold values from 0 to 1
- rewards: float32 [16], P('grp'), may hold values from -6 to 6
Outputs:
- logprobs: float32 [16, 7], P('grp')
- grad_proj: bfloat16 [2176, 4096], P('grp', 'cp')
- grad_head: bfloat16 [4096, 256], P('cp')
All inputs are finite; a program needn't handle non-finite values. No bound on the sum of `action_mask` on one device may be relied on, other than what follows from the above.
Results may differ from a plain program's by a relative error of at most 0.018.
Values may be sent and summed in bfloat16 or wider, within the bound.
A program may use at most 128 MiB of HBM per device.

v0:
```python
import math
import jax
import jax.numpy as jnp
from jax import lax
from jax.sharding import PartitionSpec as P

HD = 128
SQRT_HALF = 0.7071067811865476
INV_ROOT_TAU = 0.3989422804014327
NEG_LARGE = -1e30


def gelu_exact(values_in):
    return 0.5 * values_in * (1.0 + lax.erf(values_in * SQRT_HALF))


def gelu_slope(values_in):
    return (
        0.5 * (1.0 + lax.erf(values_in * SQRT_HALF))
        + values_in * jnp.exp(-0.5 * values_in * values_in) * INV_ROOT_TAU
    )


def fetch_columns(proj_weight):
    return lax.all_gather(proj_weight, "grp", axis=0, tiled=True)


def attention(queries, keys, values, lengths):
    episodes_here, tokens_here, att_width = queries.shape
    head_count = att_width // HD
    query_heads = queries.reshape(episodes_here, tokens_here, head_count, HD)
    key_heads = keys.reshape(episodes_here, tokens_here, head_count, HD)
    value_heads = values.reshape(episodes_here, tokens_here, head_count, HD)
    query_all, key_all, value_all = (
        lax.all_to_all(query_heads, "cp", split_axis=2, concat_axis=1, tiled=True),
        lax.all_to_all(key_heads, "cp", split_axis=2, concat_axis=1, tiled=True),
        lax.all_to_all(value_heads, "cp", split_axis=2, concat_axis=1, tiled=True),
    )
    seq_span = query_all.shape[1]
    scores = jnp.einsum(
        "eihd,ejhd->ehij", query_all, key_all, preferred_element_type=jnp.float32
    ) / math.sqrt(HD)
    live_keys = (jnp.arange(seq_span, dtype=jnp.int32)[None, :] < lengths[:, None])[
        :, None, None, :
    ]
    scores = jnp.where(live_keys, scores, NEG_LARGE)
    row_max = jnp.max(scores, axis=-1, keepdims=True)
    probs = jnp.where(live_keys, jnp.exp(scores - row_max), 0.0)
    row_total = jnp.sum(probs, axis=-1)
    weighted = jnp.einsum(
        "ehij,ejhd->eihd", probs.astype(jnp.bfloat16), value_all, preferred_element_type=jnp.float32
    )
    output = (weighted / jnp.transpose(row_total, (0, 2, 1))[..., None]).astype(jnp.bfloat16)
    returned = lax.all_to_all(output, "cp", split_axis=1, concat_axis=2, tiled=True)
    return returned.reshape(episodes_here, tokens_here, att_width)


def per_device(
    queries,
    keys,
    values,
    lengths,
    frame_map,
    proj_weight,
    head_weight,
    act_embed,
    actions,
    action_mask,
    group_ids,
    rewards,
):
    episodes_here, tokens_here, att_width = queries.shape
    action_count = act_embed.shape[0]
    lengths_real = lengths.astype(jnp.float32)
    attended = attention(queries, keys, values, lengths)
    proj_cols = fetch_columns(proj_weight)
    frames = jnp.dot(
        attended.reshape(episodes_here * tokens_here, att_width),
        frame_map,
        preferred_element_type=jnp.float32,
    )
    frames = frames.astype(jnp.bfloat16).reshape(episodes_here, tokens_here, frame_map.shape[1])
    all_frames = lax.all_gather(frames, "cp", axis=1, tiled=True)
    seq_span = all_frames.shape[1]
    flat_frames = all_frames.reshape(episodes_here * seq_span, all_frames.shape[2])
    col_count = proj_cols.shape[1]
    pre_act = jnp.dot(flat_frames, proj_cols, preferred_element_type=jnp.float32).reshape(
        episodes_here, seq_span, col_count
    )
    hidden = gelu_exact(pre_act)
    token_mask = (jnp.arange(seq_span, dtype=jnp.int32)[None, :] < lengths[:, None]).astype(
        jnp.float32
    )
    pooled = jnp.sum(token_mask[:, :, None] * hidden, axis=1) / lengths_real[:, None]
    sum_input = pooled[:, None, :] + act_embed[None, :, :]
    head_input = sum_input.astype(jnp.bfloat16).reshape(episodes_here * action_count, col_count)
    partial_logits = jnp.dot(head_input, head_weight, preferred_element_type=jnp.float32)
    episodes_total = episodes_here * lax.axis_size("grp")
    group_count = max(1, episodes_total // 8)
    membership = (group_ids[:, None] == jnp.arange(group_count, dtype=jnp.int32)[None, :]).astype(
        jnp.float32
    )
    masked = action_mask.astype(jnp.float32)
    logits = lax.psum(partial_logits, "cp")
    reward_sums, squares, group_sizes, mask_total = lax.psum(
        (
            jnp.sum(membership * rewards[:, None], axis=0),
            jnp.sum(membership * (rewards * rewards)[:, None], axis=0),
            jnp.sum(membership, axis=0),
            jnp.sum(masked),
        ),
        "grp",
    )
    log_all = jax.nn.log_softmax(logits, axis=-1)
    bin_ids = jnp.arange(head_weight.shape[1], dtype=jnp.int32)
    picked = (actions.reshape(-1)[:, None] == bin_ids[None, :]).astype(jnp.float32)
    logprobs = jnp.sum(picked * log_all, axis=-1).reshape(episodes_here, action_count)
    size_floor = jnp.maximum(group_sizes, 1.0)
    group_mean = reward_sums / size_floor
    variance = squares / size_floor - group_mean * group_mean
    group_scale = jnp.sqrt(jnp.maximum(variance, 1.0))
    advantage = (rewards - jnp.sum(membership * group_mean[None, :], axis=1)) / jnp.sum(
        membership * group_scale[None, :], axis=1
    )
    loss_weight = (-masked * advantage[:, None] / jnp.maximum(mask_total, 1.0)).reshape(-1)
    logit_grad = (loss_weight[:, None] * (picked - jnp.exp(log_all))).astype(jnp.bfloat16)
    head_term = lax.dot_general(
        head_input, logit_grad, (((0,), (0,)), ((), ())), preferred_element_type=jnp.float32
    )
    grad_head = lax.psum(head_term.astype(jnp.bfloat16), "grp")
    pull_back = lax.dot_general(
        logit_grad, head_weight, (((1,), (1,)), ((), ())), preferred_element_type=jnp.float32
    )
    pool_grad = jnp.sum(pull_back.reshape(episodes_here, action_count, col_count), axis=1)
    scaled_mask = token_mask / lengths_real[:, None]
    act_grad = (scaled_mask[:, :, None] * pool_grad[:, None, :] * gelu_slope(pre_act)).astype(
        jnp.bfloat16
    )
    act_flat = act_grad.reshape(episodes_here * seq_span, col_count)
    grad_proj = lax.psum_scatter(
        lax.dot_general(
            flat_frames, act_flat, (((0,), (0,)), ((), ())), preferred_element_type=jnp.float32
        ).astype(jnp.bfloat16),
        "grp",
        scatter_dimension=0,
        tiled=True,
    )
    return (logprobs, grad_proj, grad_head)


def solution(mesh):
    in_specs = (
        P("grp", "cp", None),
        P("grp", "cp", None),
        P("grp", "cp", None),
        P("grp"),
        P(),
        P("grp", "cp"),
        P("cp", None),
        P(None, "cp"),
        P("grp", None),
        P("grp", None),
        P("grp"),
        P("grp"),
    )
    out_specs = (P("grp", None), P("grp", "cp"), P("cp", None))
    return jax.shard_map(
        per_device, mesh=mesh, in_specs=in_specs, out_specs=out_specs, check_vma=False
    )
```

profile of v0, /device:TPU:0, one launch (start us, length us, event | category | flops | bytes accessed | tf_op | source)
XLA Modules:
  0.0 302.5 jit_solution(11430559681268954911)
XLA Ops:
  7.2 0.7 all-gather.5.cloned.1.call-update
  7.9 1.6 copy.51
  9.5 1.0 copy.52
  10.6 5.2 %all-to-all-start = ((bf16[2,128,16,128]{1,3,0,2:T(8,128)(2,1)}), bf16[2,128,16,128]{1,3,0,2:T(8,128)(2,1)S(1)}, u32[]{:S(2)}, u32[]{:S(2)}) async-start(bf16[2,128,16,128]{1,3,0,2:T(8,128)(2,1)} %copy.52), calls=%async_computation | async-start | bytes 2097152 | tf_op jit(solution)/shard_map/all_to_all | solution.py:35
  15.8 1.6 copy.55
  17.4 1.1 copy.56
  18.5 10.9 %all-to-all-done = bf16[2,128,16,128]{1,3,0,2:T(8,128)(2,1)S(1)} async-done(((bf16[2,128,16,128]{1,3,0,2:T(8,128)(2,1)}), bf16[2,128,16,128]{1,3,0,2:T(8,128)(2,1)S(1)}, u32[]{:S(2)}, u32[]{:S(2)}) %all-to-all-start) | async-done | bytes 1048608 | tf_op jit(solution)/shard_map/all_to_all | solution.py:35
  29.4 3.5 %all-to-all-start.1 = ((bf16[2,128,16,128]{1,3,0,2:T(8,128)(2,1)}), bf16[2,128,16,128]{1,3,0,2:T(8,128)(2,1)S(1)}, u32[]{:S(2)}, u32[]{:S(2)}) async-start(bf16[2,128,16,128]{1,3,0,2:T(8,128)(2,1)} %copy.56), calls=%async_computation.1 | async-start | bytes 2097152 | tf_op jit(solution)/shard_map/all_to_all | solution.py:36
  32.9 2.3 copy.59
  35.2 2.3 copy.60
  37.5 8.6 %all-to-all-done.1 = bf16[2,128,16,128]{1,3,0,2:T(8,128)(2,1)S(1)} async-done(((bf16[2,128,16,128]{1,3,0,2:T(8,128)(2,1)}), bf16[2,128,16,128]{1,3,0,2:T(8,128)(2,1)S(1)}, u32[]{:S(2)}, u32[]{:S(2)}) %all-to-all-start.1) | async-done | bytes 1048608 | tf_op jit(solution)/shard_map/all_to_all | solution.py:36
  46.2 4.3 %all-to-all-start.2 = ((bf16[2,128,16,128]{1,3,0,2:T(8,128)(2,1)}), bf16[2,128,16,128]{1,3,0,2:T(8,128)(2,1)}, u32[]{:S(2)}, u32[]{:S(2)}) async-start(bf16[2,128,16,128]{1,3,0,2:T(8,128)(2,1)} %copy.60), calls=%async_computation.2 | async-start | bytes 2097152 | tf_op jit(solution)/shard_map/all_to_all | solution.py:37
  50.6 1.3 copy.54
  51.9 1.4 copy.58
  53.2 10.5 %all-to-all-done.2 = bf16[2,128,16,128]{1,3,0,2:T(8,128)(2,1)} async-done(((bf16[2,128,16,128]{1,3,0,2:T(8,128)(2,1)}), bf16[2,128,16,128]{1,3,0,2:T(8,128)(2,1)}, u32[]{:S(2)}, u32[]{:S(2)}) %all-to-all-start.2) | async-done | bytes 1048608 | tf_op jit(solution)/shard_map/all_to_all | solution.py:37
  63.7 1.6 copy.62
  65.4 6.8 %fusion.33 = (f32[2,4,512]{2,1,0:T(4,128)S(1)}, bf16[2,4,512,512]{2,3,1,0:T(8,128)(2,1)}) fusion(pred[2,512]{1,0:T(4,128)(4,1)S(1)} %get-tuple-element.15, bf16[2,512,4,128]{3,1,2,0:T(8,128)(2,1)S(1)} %bitcast.54, bf16[2,512,4,128]{3,1,2,0:T(8,128)(2,1)} %bitcast.55), kind=kOutput, calls=%fused_computation.58 | convolution fusion | flops 549454336 | bytes 6308864 | tf_op jit(solution)/shard_map/sub | solution.py:48
  72.2 3.9 %fusion.16 = bf16[2,512,4,128]{3,1,2,0:T(8,128)(2,1)S(1)} fusion(bf16[2,512,4,128]{3,1,2,0:T(8,128)(2,1)S(1)} %bitcast.56, bf16[2,4,512,512]{2,3,1,0:T(8,128)(2,1)} %get-tuple-element.17, f32[2,512,4]{1,2,0:T(4,128)S(1)} %bitcast.57), kind=kOutput, calls=%fused_computation.23 | convolution fusion | flops 537919488 | bytes 6307840 | tf_op jit(solution)/shard_map/ehij,ejhd->eihd/dot_general | solution.py:50
  76.1 0.8 copy.64
  76.9 16.1 %all_to_all.69 = bf16[2,512,4,128]{3,2,0,1:T(4,128)(2,1)S(1)} all-to-all(bf16[2,512,4,128]{3,2,0,1:T(4,128)(2,1)S(1)} %copy.64), channel_id=1, replica_groups=mesh['cp'=4,'grp'=8] {'cp'}, dimensions={1} | all-to-all | bytes 2097152 | tf_op jit(solution)/shard_map/all_to_all | solution.py:54
  93.4 0.8 reshape_reshape.3
  94.3 7.2 %convolution_convert_fusion = bf16[256,2176]{1,0:T(8,128)(2,1)} fusion(bf16[256,2048]{1,0:T(8,128)(2,1)S(1)} %reshape_reshape.3, bf16[2048,2176]{1,0:T(8,128)(2,1)} %param.16), kind=kOutput, calls=%fused_computation.21 | convolution fusion | flops 2282258432 | bytes 11075584 | tf_op jit(solution)/shard_map/dot_general | solution.py:77
  102.3 15.2 %all-reduce = (f32[]{:T(128)}, f32[2]{0:T(128)S(1)}, f32[2]{0:T(128)S(1)}, f32[2]{0:T(128)S(1)}) all-reduce(f32[]{:T(128)} %convert_reduce_fusion.1, f32[2]{0:T(128)S(1)} %get-tuple-element.7, f32[2]{0:T(128)S(1)} %get-tuple-element.6, f32[2]{0:T(128)S(1)} %get-tuple-element.5), channel_id=1, replica_groups=mesh['cp'=4,'grp'=8] {'grp'}, use_global_device_ids=true, to_apply=%region_16.17 | all-reduce | flops 7 | bytes 56 | tf_op jit(solution)/shard_map/psum | solution.py:105
  118.7 37.5 %all-gather.3.cloned.1.call-done = bf16[2,512,2176]{2,1,0:T(8,128)(2,1)} async-done(((bf16[2,128,2176]{2,1,0:T(8,128)(2,1)}), bf16[2,512,2176]{2,1,0:T(8,128)(2,1)}) %all-gather.3.cloned.1.call-update) | async-done | bytes 4456464 | tf_op jit(solution)/shard_map/all_gather | solution.py:83
  156.2 9.9 %multiply_reduce_fusion = (f32[2,1024]{1,0:T(2,128)S(1)}, f32[2,512,1024]{2,1,0:T(8,128)}) fusion(f32[2,512]{1,0:T(2,128)S(1)} %get-tuple-element.14, bf16[2,512,2176]{2,1,0:T(8,128)(2,1)} %all-gather.3.cloned.1.call-done, bf16[2176,1024]{1,0:T(8,128)(2,1)} %all-gather.5.cloned.1.call-done), kind=kOutput, calls=%fused_computation.14 | convolution fusion | flops 4569692160 | bytes 13119488 | tf_op jit(solution)/shard_map/dot_general | solution.py:87
  166.4 15.1 %psum.42 = f32[14,256]{1,0:T(8,128)S(1)} all-reduce(f32[14,256]{1,0:T(8,128)S(1)} %fusion.34), channel_id=1, replica_groups=mesh['cp'=4,'grp'=8] {'cp'}, use_global_device_ids=true, to_apply=%region_3.4 | all-reduce | flops 3584 | bytes 28672 | tf_op jit(solution)/shard_map/psum | solution.py:104
  182.1 1.2 convolution_convert_fusion.1
  183.4 10.3 %bitcast_convert_fusion = bf16[2176,1024]{1,0:T(8,128)(2,1)} fusion(bf16[2,512,2176]{2,1,0:T(8,128)(2,1)} %all-gather.3.cloned.1.call-done, f32[2,512,1024]{2,1,0:T(8,128)} %get-tuple-element.19, f32[2,1024]{1,0:T(2,128)S(1)} %reduce_sum.110, f32[2,512]{1,0:T(2,128)S(1)} %broadcast_divide_fusion.1), kind=kOutput, calls=%fused_computation.1 | convolution fusion | flops 4577165312 | bytes 13119488 | tf_op jit(solution)/shard_map/dot_general | solution.py:141
  193.9 0.6 reshape.138
  194.5 45.4 %all-reduce.3.cloned.1.call-done = bf16[1024,256]{1,0:T(8,128)(2,1)} async-done(((bf16[1024,256]{1,0:T(8,128)(2,1)}), bf16[1024,256]{1,0:T(8,128)(2,1)}) %all-reduce.3.cloned.1.call-update) | async-done | bytes 524304 | tf_op jit(solution)/shard_map/psum | solution.py:130
  239.9 54.2 %reduce-scatter.2.cloned.1.call-done = bf16[272,1024]{1,0:T(8,128)(2,1)} async-done(((bf16[2176,1024]{1,0:T(8,128)(2,1)}), bf16[272,1024]{1,0:T(8,128)(2,1)}) %reduce-scatter.2.cloned.1.call-update) | async-done | bytes 557072 | tf_op jit(solution)/shard_map/reduce_scatter | solution.py:140
  294.1 1.9 copy.75
  (48 shorter events, 3.0 us)
Async XLA Ops:
  7.2 159.1 %copy-start = (bf16[1024,256]{1,0:T(8,128)(2,1)S(1)}, bf16[1024,256]{1,0:T(8,128)(2,1)}, u32[]{:S(2)}) copy-start(bf16[1024,256]{1,0:T(8,128)(2,1)} %param.18) | copy-start | bytes 1572868
  7.2 111.5 %all-gather.5.cloned.1.call-start = ((), (), s32[]{:S(2)}) async-start(), calls=%async_computation.6 | async-start | bytes 5013504 | tf_op jit(solution)/shard_map/all_gather | solution.py:25
  10.6 18.8 %all-to-all-start = ((bf16[2,128,16,128]{1,3,0,2:T(8,128)(2,1)}), bf16[2,128,16,128]{1,3,0,2:T(8,128)(2,1)S(1)}, u32[]{:S(2)}, u32[]{:S(2)}) async-start(bf16[2,128,16,128]{1,3,0,2:T(8,128)(2,1)} %copy.52), calls=%async_computation | async-start | bytes 2097152 | tf_op jit(solution)/shard_map/all_to_all | solution.py:35
  18.5 32.0 %copy-start.5 = (s32[2]{0:T(128)S(1)}, s32[2]{0:T(128)}, u32[]{:S(2)}) copy-start(s32[2]{0:T(128)} %param.15) | copy-start | bytes 28
  29.4 16.8 %all-to-all-start.1 = ((bf16[2,128,16,128]{1,3,0,2:T(8,128)(2,1)}), bf16[2,128,16,128]{1,3,0,2:T(8,128)(2,1)S(1)}, u32[]{:S(2)}, u32[]{:S(2)}) async-start(bf16[2,128,16,128]{1,3,0,2:T(8,128)(2,1)} %copy.56), calls=%async_computation.1 | async-start | bytes 2097152 | tf_op jit(solution)/shard_map/all_to_all | solution.py:36
  46.2 17.6 %all-to-all-start.2 = ((bf16[2,128,16,128]{1,3,0,2:T(8,128)(2,1)}), bf16[2,128,16,128]{1,3,0,2:T(8,128)(2,1)}, u32[]{:S(2)}, u32[]{:S(2)}) async-start(bf16[2,128,16,128]{1,3,0,2:T(8,128)(2,1)} %copy.60), calls=%async_computation.2 | async-start | bytes 2097152 | tf_op jit(solution)/shard_map/all_to_all | solution.py:37
  50.4 105.8 %all-gather.3.cloned.1.call-start = ((), (), s32[]{:S(2)}) async-start(), calls=%async_computation.5 | async-start | bytes 5570560 | tf_op jit(solution)/shard_map/all_gather | solution.py:83
  51.9 13.5 %copy-start.1 = (bf16[2,4,128,4,128]{4,2,1,3,0:T(8,128)(2,1)S(1)}, bf16[2,4,128,4,128]{4,2,1,3,0:T(8,128)(2,1)}, u32[]{:S(2)}) copy-start(bf16[2,4,128,4,128]{4,2,1,3,0:T(8,128)(2,1)} %copy.54) | copy-start | bytes 3145732
  94.2 7.3 %copy-start.4 = (f32[2]{0:T(128)S(1)}, f32[2]{0:T(128)}, u32[]{:S(2)}) copy-start(f32[2]{0:T(128)} %param.23) | copy-start | bytes 28
  94.2 7.4 %copy-start.6 = (s32[2,7]{1,0:T(2,128)S(1)}, s32[2,7]{1,0:T(2,128)}, u32[]{:S(2)}) copy-start(s32[2,7]{1,0:T(2,128)} %param.21) | copy-start | bytes 172
  94.2 8.0 %copy-start.3 = (s32[2]{0:T(128)S(1)}, s32[2]{0:T(128)}, u32[]{:S(2)}) copy-start(s32[2]{0:T(128)} %param.22) | copy-start | bytes 28
  94.3 23.3 %copy-start.7 = (s32[2,7]{1,0:T(2,128)S(1)}, s32[2,7]{1,0:T(2,128)}, u32[]{:S(2)}) copy-start(s32[2,7]{1,0:T(2,128)} %param.20) | copy-start | bytes 172
  101.5 138.4 %all-reduce.3.cloned.1.call-start = ((), (), s32[]{:S(2)}) async-start(), calls=%async_computation.8 | async-start | bytes 1048576 | tf_op jit(solution)/shard_map/psum | solution.py:130
  156.2 10.0 %copy-start.2 = (f32[7,1024]{1,0:T(8,128)S(1)}, f32[7,1024]{1,0:T(8,128)}, u32[]{:S(2)}) copy-start(f32[7,1024]{1,0:T(8,128)} %param.19) | copy-start | bytes 86020
  183.3 110.8 %reduce-scatter.2.cloned.1.call-start = ((), (), s32[]{:S(2)}) async-start(), calls=%async_computation.7 | async-start | bytes 5013504 | tf_op jit(solution)/shard_map/reduce_scatter | solution.py:140
Sparse Core Ops, SparseCore 0:
  9.6 51.7 all-gather.4
  101.6 54.4 all-gather.2
  183.4 56.4 all-reduce.2
  242.7 51.4 reduce-scatter.1
where the time goes:
time: 303 us
  waiting for transfers between devices  168 us (55%)
  blocking collectives  46.4 us (15%)
  matrix products  39.8 us (13%)
  local copies, waits for them, and re-layouts  19 us (6%)
  between operations  14.6 us (5%)
  starting transfers between devices  13.1 us (4%)
    reduce_scatter x1, waiting for transfers between devices, per_device(): lax.psum_scatter(lax.dot_general(flat_frames, act_flat, (((0,), (0,)), ((...  54.2 us
    psum x1, waiting for transfers between devices, per_device(): grad_head = lax.psum(head_term.astype(jnp.bfloat16), 'grp')  45.4 us
    all_gather x1, waiting for transfers between devices, per_device(): all_frames = lax.all_gather(frames, 'cp', axis=1, tiled=True)  37.5 us
    all_to_all x1, blocking collectives, attention(): lax.all_to_all(output, 'cp', split_axis=1, concat_axis=2, tiled=True)  16.1 us
    psum x1, blocking collectives, per_device(): lax.psum((jnp.sum(membership * rewards[:, None], axis=0), jnp.sum(members...  15.2 us
    psum x1, blocking collectives, per_device(): logits = lax.psum(partial_logits, 'cp')  15.1 us
    all_to_all x1, waiting for transfers between devices, attention(): lax.all_to_all(query_heads, 'cp', split_axis=2, concat_axis=1, tiled=True)  10.9 us
    all_to_all x1, waiting for transfers between devices, attention(): lax.all_to_all(value_heads, 'cp', split_axis=2, concat_axis=1, tiled=True)  10.5 us
  transfers between devices with their start and end apart: 7, of which 6 were waited for; matrix products, arithmetic and copies ran while one was open for 15% of the time, Pallas kernels for 0%

commit v1 on v0

--- a/solution.py
+++ b/solution.py
@@ -80,7 +80,8 @@
         preferred_element_type=jnp.float32,
     )
     frames = frames.astype(jnp.bfloat16).reshape(episodes_here, tokens_here, frame_map.shape[1])
-    all_frames = lax.all_gather(frames, "cp", axis=1, tiled=True)
+    blocks = lax.all_gather(frames, "cp", axis=0, tiled=False)
+    all_frames = jnp.concatenate(blocks, axis=1)
     seq_span = all_frames.shape[1]
     flat_frames = all_frames.reshape(episodes_here * seq_span, all_frames.shape[2])
     col_count = proj_cols.shape[1]

time: 303 us -> 303 us (level)
  other arithmetic: 1.73 us -> 5.74 us
    convert_element_type x0 -> x1, other arithmetic: none -> 4.01 us  [per_device(): (scaled_mask[:, :, None] * pool_grad[:, None, :] * gelu_slope(pre_act)).a...]
  transfers between devices with their start and end apart: 7 -> 7, of which waited for: 6 -> 6; matrix products, arithmetic and copies ran while one was open for 15% -> 16% of each run, Pallas kernels for 0% -> 0%
where the time goes in v1:
time: 303 us
  waiting for transfers between devices  165 us (54%)
  blocking collectives  46.4 us (15%)
  matrix products  38.4 us (13%)
  local copies, waits for them, and re-layouts  19 us (6%)
  between operations  14.6 us (5%)
  starting transfers between devices  13.1 us (4%)
  other arithmetic  5.74 us (2%)
    reduce_scatter x1, waiting for transfers between devices, per_device(): lax.psum_scatter(lax.dot_general(flat_frames, act_flat, (((0,), (0,)), ((...  54.2 us
    psum x1, waiting for transfers between devices, per_device(): grad_head = lax.psum(head_term.astype(jnp.bfloat16), 'grp')  42.9 us
    all_gather x1, waiting for transfers between devices, per_device(): blocks = lax.all_gather(frames, 'cp', axis=0, tiled=False)  37.5 us
    all_to_all x1, blocking collectives, attention(): lax.all_to_all(output, 'cp', split_axis=1, concat_axis=2, tiled=True)  16.1 us
    psum x1, blocking collectives, per_device(): lax.psum((jnp.sum(membership * rewards[:, None], axis=0), jnp.sum(members...  15.2 us
    psum x1, blocking collectives, per_device(): logits = lax.psum(partial_logits, 'cp')  15.1 us
    all_to_all x1, waiting for transfers between devices, attention(): lax.all_to_all(value_heads, 'cp', split_axis=2, concat_axis=1, tiled=True)  11 us
    all_to_all x1, waiting for transfers between devices, attention(): lax.all_to_all(key_heads, 'cp', split_axis=2, concat_axis=1, tiled=True)  10.5 us
  transfers between devices with their start and end apart: 7, of which 6 were waited for; matrix products, arithmetic and copies ran while one was open for 16% of the time, Pallas kernels for 0%

profile of v1, /device:TPU:0, one launch (start us, length us, event | category | flops | bytes accessed | tf_op | source)
XLA Modules:
  0.0 302.6 jit_solution(17193684282912918958)
XLA Ops:
  7.2 0.7 all-gather.5.cloned.1.call-update
  7.9 1.6 copy.59
  9.5 1.1 copy.60
  10.6 5.2 %all-to-all-start.2 = ((bf16[2,128,16,128]{1,3,0,2:T(8,128)(2,1)}), bf16[2,128,16,128]{1,3,0,2:T(8,128)(2,1)S(1)}, u32[]{:S(2)}, u32[]{:S(2)}) async-start(bf16[2,128,16,128]{1,3,0,2:T(8,128)(2,1)} %copy.60), calls=%async_computation.2 | async-start | bytes 2097152 | tf_op jit(solution)/shard_map/all_to_all | solution.py:37
  15.8 1.6 copy.51
  17.4 1.0 copy.52
  18.5 11.0 %all-to-all-done.2 = bf16[2,128,16,128]{1,3,0,2:T(8,128)(2,1)S(1)} async-done(((bf16[2,128,16,128]{1,3,0,2:T(8,128)(2,1)}), bf16[2,128,16,128]{1,3,0,2:T(8,128)(2,1)S(1)}, u32[]{:S(2)}, u32[]{:S(2)}) %all-to-all-start.2) | async-done | bytes 1048608 | tf_op jit(solution)/shard_map/all_to_all | solution.py:37
  29.4 3.5 %all-to-all-start = ((bf16[2,128,16,128]{1,3,0,2:T(8,128)(2,1)}), bf16[2,128,16,128]{1,3,0,2:T(8,128)(2,1)S(1)}, u32[]{:S(2)}, u32[]{:S(2)}) async-start(bf16[2,128,16,128]{1,3,0,2:T(8,128)(2,1)} %copy.52), calls=%async_computation | async-start | bytes 2097152 | tf_op jit(solution)/shard_map/all_to_all | solution.py:35
  33.0 2.3 copy.55
  35.2 2.3 copy.56
  37.6 8.6 %all-to-all-done = bf16[2,128,16,128]{1,3,0,2:T(8,128)(2,1)S(1)} async-done(((bf16[2,128,16,128]{1,3,0,2:T(8,128)(2,1)}), bf16[2,128,16,128]{1,3,0,2:T(8,128)(2,1)S(1)}, u32[]{:S(2)}, u32[]{:S(2)}) %all-to-all-start) | async-done | bytes 1048608 | tf_op jit(solution)/shard_map/all_to_all | solution.py:35
  46.2 4.2 %all-to-all-start.1 = ((bf16[2,128,16,128]{1,3,0,2:T(8,128)(2,1)}), bf16[2,128,16,128]{1,3,0,2:T(8,128)(2,1)}, u32[]{:S(2)}, u32[]{:S(2)}) async-start(bf16[2,128,16,128]{1,3,0,2:T(8,128)(2,1)} %copy.56), calls=%async_computation.1 | async-start | bytes 2097152 | tf_op jit(solution)/shard_map/all_to_all | solution.py:36
  50.6 1.3 copy.62
  51.9 1.3 copy.54
  53.2 10.5 %all-to-all-done.1 = bf16[2,128,16,128]{1,3,0,2:T(8,128)(2,1)} async-done(((bf16[2,128,16,128]{1,3,0,2:T(8,128)(2,1)}), bf16[2,128,16,128]{1,3,0,2:T(8,128)(2,1)}, u32[]{:S(2)}, u32[]{:S(2)}) %all-to-all-start.1) | async-done | bytes 1048608 | tf_op jit(solution)/shard_map/all_to_all | solution.py:36
  63.8 1.6 copy.58
  65.4 6.9 %fusion.24 = (f32[2,4,512]{2,1,0:T(4,128)S(1)}, bf16[2,4,512,512]{2,3,1,0:T(8,128)(2,1)}) fusion(pred[2,512]{1,0:T(4,128)(4,1)S(1)} %get-tuple-element.15, bf16[2,512,4,128]{3,1,2,0:T(8,128)(2,1)} %bitcast.63, bf16[2,512,4,128]{3,1,2,0:T(8,128)(2,1)S(1)} %bitcast.64), kind=kOutput, calls=%fused_computation.50 | convolution fusion | flops 549454336 | bytes 6308864 | tf_op jit(solution)/shard_map/sub | solution.py:48
  72.3 3.9 %fusion.15 = bf16[2,512,4,128]{3,1,2,0:T(8,128)(2,1)S(1)} fusion(bf16[2,512,4,128]{3,1,2,0:T(8,128)(2,1)S(1)} %bitcast.62, bf16[2,4,512,512]{2,3,1,0:T(8,128)(2,1)} %get-tuple-element.17, f32[2,512,4]{1,2,0:T(4,128)S(1)} %bitcast.67), kind=kOutput, calls=%fused_computation.23 | convolution fusion | flops 537919488 | bytes 6307840 | tf_op jit(solution)/shard_map/ehij,ejhd->eihd/dot_general | solution.py:50
  76.2 0.8 copy.64
  77.0 16.1 %all_to_all.69 = bf16[2,512,4,128]{3,2,0,1:T(4,128)(2,1)S(1)} all-to-all(bf16[2,512,4,128]{3,2,0,1:T(4,128)(2,1)S(1)} %copy.64), channel_id=1, replica_groups=mesh['cp'=4,'grp'=8] {'cp'}, dimensions={1} | all-to-all | bytes 2097152 | tf_op jit(solution)/shard_map/all_to_all | solution.py:54
  93.5 0.8 reshape_reshape.6
  94.4 7.2 %convolution_convert_fusion.1 = bf16[256,2176]{1,0:T(8,128)(2,1)} fusion(bf16[256,2048]{1,0:T(8,128)(2,1)S(1)} %reshape_reshape.6, bf16[2048,2176]{1,0:T(8,128)(2,1)} %param.16), kind=kOutput, calls=%fused_computation.21 | convolution fusion | flops 2282258432 | bytes 11075584 | tf_op jit(solution)/shard_map/dot_general | solution.py:77
  102.4 15.2 %all-reduce = (f32[]{:T(128)}, f32[2]{0:T(128)S(1)}, f32[2]{0:T(128)S(1)}, f32[2]{0:T(128)S(1)}) all-reduce(f32[]{:T(128)} %convert_reduce_fusion.1, f32[2]{0:T(128)S(1)} %get-tuple-element.7, f32[2]{0:T(128)S(1)} %get-tuple-element.6, f32[2]{0:T(128)S(1)} %get-tuple-element.5), channel_id=1, replica_groups=mesh['cp'=4,'grp'=8] {'grp'}, use_global_device_ids=true, to_apply=%region_16.17 | all-reduce | flops 7 | bytes 56 | tf_op jit(solution)/shard_map/psum | solution.py:106
  118.8 37.5 %all-gather.3.cloned.1.call-done = bf16[4,2,128,2176]{3,2,0,1:T(8,128)(2,1)} async-done(((bf16[1,2,128,2176]{3,2,0,1:T(8,128)(2,1)}), bf16[4,2,128,2176]{3,2,0,1:T(8,128)(2,1)}) %all-gather.3.cloned.1.call-update) | async-done | bytes 4456464 | tf_op jit(solution)/shard_map/all_gather | solution.py:83
  156.3 9.9 %multiply_reduce_fusion = (f32[2,1024]{1,0:T(2,128)S(1)}, f32[2,512,1024]{2,1,0:T(8,128)}) fusion(f32[2,512]{1,0:T(2,128)S(1)} %get-tuple-element.14, bf16[2,512,2176]{2,1,0:T(8,128)(2,1)} %bitcast.65, bf16[2176,1024]{1,0:T(8,128)(2,1)} %all-gather.5.cloned.1.call-done), kind=kOutput, calls=%fused_computation.14 | convolution fusion | flops 4569692160 | bytes 13119488 | tf_op jit(solution)/shard_map/dot_general | solution.py:88
  166.5 15.1 %psum.42 = f32[14,256]{1,0:T(8,128)S(1)} all-reduce(f32[14,256]{1,0:T(8,128)S(1)} %fusion.25), channel_id=1, replica_groups=mesh['cp'=4,'grp'=8] {'cp'}, use_global_device_ids=true, to_apply=%region_3.4 | all-reduce | flops 3584 | bytes 28672 | tf_op jit(solution)/shard_map/psum | solution.py:105
  182.2 1.2 convolution_convert_fusion.2
  183.5 4.0 %fusion.9 = bf16[2,512,1024]{2,1,0:T(8,128)(2,1)S(1)} fusion(f32[2,512,1024]{2,1,0:T(8,128)} %get-tuple-element.19, f32[2,1024]{1,0:T(2,128)S(1)} %reduce_sum.110, f32[2,512]{1,0:T(2,128)S(1)} %broadcast_divide_fusion.1), kind=kLoop, calls=%fused_computation.13 | loop fusion | flops 11534336 | bytes 6303744 | tf_op jit(solution)/shard_map/convert_element_type | solution.py:137
  187.5 8.8 %convolution_convert_fusion = bf16[2176,1024]{1,0:T(8,128)(2,1)} fusion(bf16[1024,2176]{1,0:T(8,128)(2,1)} %bitcast.66, bf16[1024,1024]{1,0:T(8,128)(2,1)S(1)} %bitcast.60), kind=kOutput, calls=%fused_computation.5 | convolution fusion | flops 4565630976 | bytes 11010048 | tf_op jit(solution)/shard_map/dot_general | solution.py:142
  197.1 42.9 %all-reduce.3.cloned.1.call-done = bf16[1024,256]{1,0:T(8,128)(2,1)} async-done(((bf16[1024,256]{1,0:T(8,128)(2,1)}), bf16[1024,256]{1,0:T(8,128)(2,1)}) %all-reduce.3.cloned.1.call-update) | async-done | bytes 524304 | tf_op jit(solution)/shard_map/psum | solution.py:131
  240.0 54.2 %reduce-scatter.2.cloned.1.call-done = bf16[272,1024]{1,0:T(8,128)(2,1)} async-done(((bf16[2176,1024]{1,0:T(8,128)(2,1)}), bf16[272,1024]{1,0:T(8,128)(2,1)}) %reduce-scatter.2.cloned.1.call-update) | async-done | bytes 557072 | tf_op jit(solution)/shard_map/reduce_scatter | solution.py:141
  294.2 1.9 copy.74
  (49 shorter events, 3.6 us)
Async XLA Ops:
  7.2 159.2 %copy-start = (bf16[1024,256]{1,0:T(8,128)(2,1)S(1)}, bf16[1024,256]{1,0:T(8,128)(2,1)}, u32[]{:S(2)}) copy-start(bf16[1024,256]{1,0:T(8,128)(2,1)} %param.18) | copy-start | bytes 1572868
  7.2 111.6 %all-gather.5.cloned.1.call-start = ((), (), s32[]{:S(2)}) async-start(), calls=%async_computation.6 | async-start | bytes 5013504 | tf_op jit(solution)/shard_map/all_gather | solution.py:25
  10.6 18.8 %all-to-all-start.2 = ((bf16[2,128,16,128]{1,3,0,2:T(8,128)(2,1)}), bf16[2,128,16,128]{1,3,0,2:T(8,128)(2,1)S(1)}, u32[]{:S(2)}, u32[]{:S(2)}) async-start(bf16[2,128,16,128]{1,3,0,2:T(8,128)(2,1)} %copy.60), calls=%async_computation.2 | async-start | bytes 2097152 | tf_op jit(solution)/shard_map/all_to_all | solution.py:37
  18.5 32.0 %copy-start.5 = (s32[2]{0:T(128)S(1)}, s32[2]{0:T(128)}, u32[]{:S(2)}) copy-start(s32[2]{0:T(128)} %param.15) | copy-start | bytes 28
  29.4 16.8 %all-to-all-start = ((bf16[2,128,16,128]{1,3,0,2:T(8,128)(2,1)}), bf16[2,128,16,128]{1,3,0,2:T(8,128)(2,1)S(1)}, u32[]{:S(2)}, u32[]{:S(2)}) async-start(bf16[2,128,16,128]{1,3,0,2:T(8,128)(2,1)} %copy.52), calls=%async_computation | async-start | bytes 2097152 | tf_op jit(solution)/shard_map/all_to_all | solution.py:35
  46.2 17.6 %all-to-all-start.1 = ((bf16[2,128,16,128]{1,3,0,2:T(8,128)(2,1)}), bf16[2,128,16,128]{1,3,0,2:T(8,128)(2,1)}, u32[]{:S(2)}, u32[]{:S(2)}) async-start(bf16[2,128,16,128]{1,3,0,2:T(8,128)(2,1)} %copy.56), calls=%async_computation.1 | async-start | bytes 2097152 | tf_op jit(solution)/shard_map/all_to_all | solution.py:36
  50.4 105.8 %all-gather.3.cloned.1.call-start = ((), (), s32[]{:S(2)}) async-start(), calls=%async_computation.5 | async-start | bytes 5570560 | tf_op jit(solution)/shard_map/all_gather | solution.py:83
  65.4 6.9 %copy-start.1 = (bf16[2,4,128,4,128]{4,2,1,3,0:T(8,128)(2,1)S(1)}, bf16[2,4,128,4,128]{4,2,1,3,0:T(8,128)(2,1)}, u32[]{:S(2)}) copy-start(bf16[2,4,128,4,128]{4,2,1,3,0:T(8,128)(2,1)} %copy.62) | copy-start | bytes 3145732
  94.3 7.3 %copy-start.4 = (f32[2]{0:T(128)S(1)}, f32[2]{0:T(128)}, u32[]{:S(2)}) copy-start(f32[2]{0:T(128)} %param.23) | copy-start | bytes 28
  94.3 7.4 %copy-start.6 = (s32[2,7]{1,0:T(2,128)S(1)}, s32[2,7]{1,0:T(2,128)}, u32[]{:S(2)}) copy-start(s32[2,7]{1,0:T(2,128)} %param.21) | copy-start | bytes 172
  94.3 8.0 %copy-start.3 = (s32[2]{0:T(128)S(1)}, s32[2]{0:T(128)}, u32[]{:S(2)}) copy-start(s32[2]{0:T(128)} %param.22) | copy-start | bytes 28
  94.4 23.2 %copy-start.7 = (s32[2,7]{1,0:T(2,128)S(1)}, s32[2,7]{1,0:T(2,128)}, u32[]{:S(2)}) copy-start(s32[2,7]{1,0:T(2,128)} %param.20) | copy-start | bytes 172
  101.6 138.4 %all-reduce.3.cloned.1.call-start = ((), (), s32[]{:S(2)}) async-start(), calls=%async_computation.8 | async-start | bytes 1048576 | tf_op jit(solution)/shard_map/psum | solution.py:131
  156.3 10.0 %copy-start.2 = (f32[7,1024]{1,0:T(8,128)S(1)}, f32[7,1024]{1,0:T(8,128)}, u32[]{:S(2)}) copy-start(f32[7,1024]{1,0:T(8,128)} %param.19) | copy-start | bytes 86020
  183.4 110.8 %reduce-scatter.2.cloned.1.call-start = ((), (), s32[]{:S(2)}) async-start(), calls=%async_computation.7 | async-start | bytes 5013504 | tf_op jit(solution)/shard_map/reduce_scatter | solution.py:141
Sparse Core Ops, SparseCore 0:
  9.6 51.7 all-gather.4
  101.7 54.4 all-gather.2
  183.5 56.4 all-reduce.2
  242.7 51.4 reduce-scatter.1
